TPU v7x, 256 devices: a whole 4x4x8 slice. The times are simulated.
256 devices in a mesh: dp: 4 (over x), expert: 64 (over y, z, core).
Axes of the slice: x: 4, y: 4, z: 8, core: 2. Of those that a mesh axis runs over, the one named last changes fastest.
Arguments:
- tokens: bfloat16 [8192, 2048], P('expert'), may hold values from -4 to 4
- norm_gain: bfloat16 [2048], replicated, may hold values from 0.5 to 1.5
- routing_projection_matrix: bfloat16 [2048, 64], replicated, may hold values from -0.125 to 0.125
- experts: int32 [8192, 8], P('expert'), may hold values from 0 to 63, as said below
- replica_key: int32 [8192, 8], P('expert'), may hold values from 0 to 1048575
- slot_expert: int32 [128], replicated, may hold values from 0 to 63, as said below
- capacity: int32 [128], replicated, may hold values from 4 to 16, as said below
- slot_gate_up_weight: bfloat16 [128, 2048, 2, 1024], P('expert', None, None, 'dp'), may hold values from -0.125 to 0.125
- down_weight: bfloat16 [128, 1024, 2048], P('expert', 'dp'), may hold values from -0.1875 to 0.1875
Outputs:
- mixed: bfloat16 [8192, 2048], P('expert', 'dp')
Inputs may be any that keep to these rules, and one draw needn't show every extreme that they name: Each row names 8 different experts. `slot_expert`: every expert occupies at least one slot. `capacity`: for every j the capacities of slots 2 * j and 2 * j + 1 sum to at most 24, and to exactly 24 for some j.
All inputs are finite; a program needn't handle non-finite values.
Results may differ from a plain program's by a relative error of at most 0.012.
Values may be sent and summed in bfloat16 or wider, within the bound.
A program may use at most 128 MiB of HBM per device.

v0:
```python
import jax
import jax.numpy as jnp
from jax import lax
from jax.sharding import PartitionSpec as P

CAPACITY_HIGH = 16
CAP_DEV = 24


def assign_slots(experts, replica_key, slot_expert):
    flat_experts = experts.reshape(-1)
    holders = (flat_experts[:, None] == slot_expert[None, :]).astype(jnp.int32)
    copies = jnp.sum(holders, axis=1)
    earlier = jnp.cumsum(holders, axis=1) - holders
    wanted = replica_key.reshape(-1) % copies
    matched = holders * (earlier == wanted[:, None]).astype(jnp.int32)
    numbers = jnp.arange(slot_expert.shape[0], dtype=jnp.int32)
    return jnp.sum(matched * numbers[None, :], axis=1)


def slot_partial(flat_rows, gate_up_one, down_one):
    model_width = flat_rows.shape[1]
    unit_count = gate_up_one.shape[2]
    gate_up_out = jnp.dot(
        flat_rows,
        gate_up_one.reshape(model_width, 2 * unit_count),
        preferred_element_type=jnp.float32,
    )
    activated = (jax.nn.silu(gate_up_out[:, :unit_count]) * gate_up_out[:, unit_count:]).astype(
        jnp.bfloat16
    )
    result = jnp.dot(activated, down_one, preferred_element_type=jnp.float32)
    return result.astype(jnp.bfloat16)


def on_device(
    tokens,
    norm_gain,
    routing_projection_matrix,
    experts,
    replica_key,
    slot_expert,
    capacity,
    slot_gate_up_weight,
    down_weight,
):
    peer_count = lax.axis_size("expert")
    group_count = lax.axis_size("dp")
    group_pos = lax.axis_index("dp")
    me = lax.axis_index("expert")
    rows_here = tokens.shape[0]
    model_width = tokens.shape[1]
    pick_count = experts.shape[1]
    slot_count = slot_expert.shape[0]
    per_device = slot_count // peer_count
    quarter = model_width // group_count
    buffer_rows = CAP_DEV
    hidden = tokens.astype(jnp.float32)
    scale = lax.rsqrt(jnp.mean(hidden * hidden, axis=-1, keepdims=True) + 1e-06)
    normed = (hidden * scale * norm_gain.astype(jnp.float32)).astype(jnp.bfloat16)
    logits = jnp.dot(normed, routing_projection_matrix, preferred_element_type=jnp.float32)
    score = jax.nn.sigmoid(jnp.take_along_axis(logits, experts, axis=1)).reshape(-1)
    slot_ids = assign_slots(experts, replica_key, slot_expert)
    onehot = (slot_ids[:, None] == jnp.arange(slot_count, dtype=jnp.int32)[None, :]).astype(
        jnp.int32
    )
    position = jnp.sum((jnp.cumsum(onehot, axis=0) - onehot) * onehot, axis=1)
    slot_cap = jnp.sum(onehot * capacity[None, :], axis=1)
    kept_mask = position < slot_cap
    is_second = slot_ids % per_device == 1
    row_in = jnp.where(is_second, buffer_rows - slot_cap + position, position)
    target = jnp.where(
        kept_mask, slot_ids // per_device * buffer_rows + row_in, peer_count * buffer_rows
    )
    source_rows = jnp.arange(rows_here * pick_count, dtype=jnp.int32) // pick_count
    normed_part = lax.dynamic_slice_in_dim(normed, group_pos * quarter, quarter, 1)
    outgoing = (
        jnp.zeros((peer_count * buffer_rows + 1, quarter), jnp.bfloat16)
        .at[target]
        .set(normed_part[source_rows])
    )
    outgoing = outgoing[:-1].reshape(peer_count, buffer_rows, quarter)
    incoming_part = lax.all_to_all(outgoing, "expert", split_axis=0, concat_axis=0, tiled=True)
    incoming = lax.all_gather(incoming_part, "dp", axis=2, tiled=True)
    flat_in = incoming.reshape(peer_count * buffer_rows, model_width)
    first_out = slot_partial(flat_in, slot_gate_up_weight[0], down_weight[0])
    second_out = slot_partial(flat_in, slot_gate_up_weight[1], down_weight[1])
    first_cap = lax.dynamic_index_in_dim(capacity, me * per_device, keepdims=False)
    row_index = jnp.arange(peer_count * buffer_rows, dtype=jnp.int32) % buffer_rows
    partial_value = jnp.where((row_index < first_cap)[:, None], first_out, second_out)
    partial_value = partial_value.reshape(peer_count, buffer_rows, model_width)
    summed = lax.psum_scatter(partial_value, "dp", scatter_dimension=2, tiled=True)
    returned = lax.all_to_all(summed, "expert", split_axis=0, concat_axis=0, tiled=True)
    flat_ret = returned.reshape(peer_count * buffer_rows, quarter)
    flat_ret = jnp.concatenate([flat_ret, jnp.zeros((1, quarter), flat_ret.dtype)])
    weight_kept = jnp.where(kept_mask, score, jnp.float32(0.0))
    gathered = flat_ret[target].astype(jnp.float32).reshape(rows_here, pick_count, quarter)
    mixture = jnp.sum(weight_kept.reshape(rows_here, pick_count)[:, :, None] * gathered, axis=1)
    residual = lax.dynamic_slice_in_dim(tokens, group_pos * quarter, quarter, 1).astype(jnp.float32)
    return (residual + mixture).astype(jnp.bfloat16)


def solution(mesh):
    in_specs = (
        P("expert", None),
        P(),
        P(),
        P("expert", None),
        P("expert", None),
        P(),
        P(),
        P("expert", None, None, "dp"),
        P("expert", "dp", None),
    )
    out_specs = P("expert", "dp")
    return jax.shard_map(
        on_device, mesh=mesh, in_specs=in_specs, out_specs=out_specs, check_vma=False
    )
```

profile of v0, /device:TPU:1, one launch (start us, length us, event | category | flops | bytes accessed | tf_op | source)
XLA Modules:
  0.0 289.3 jit_solution(4413022350040989855)
XLA Ops:
  6.6 0.8 copy.21
  7.4 0.1 eq.65
  7.5 0.8 convert_reduce_fusion
  8.3 0.8 compare_convert_fusion
  9.0 1.2 fusion.3
  10.3 0.7 convert_element_type.50
  11.0 0.8 copy.22
  11.8 0.1 reshape.250
  11.9 0.5 reduce_window_sum.26
  12.4 0.1 add_select_fusion.1
  12.5 0.2 fusion.19
  12.7 0.1 copy.23
  12.8 0.2 fusion.23
  13.1 0.3 copy.24
  13.4 0.2 fusion.5
  13.6 0.2 select_reduce_fusion
  13.9 0.5 copy-done.2
  14.4 10.1 %scatter_custom_fusion = bf16[1537,512]{1,0:T(8,128)(2,1)S(1)} fusion(s32[1024]{0:T(1024)S(1)} %bitcast.69, bf16[128,512]{1,0:T(8,128)(2,1)S(1)} %constant_dynamic-slice_fusion, s32[1024]{0:T(1024)S(1)} %broadcast_clamp_fusion.1, bf16[]{:T(256)} %constant.114.clone.1), kind=kCustom, calls=%fused_computation.20 | custom fusion | bytes 1573890 | tf_op jit(solution)/shard_map/scatter | solution.py:80
  24.5 0.1 slice.52
  24.6 52.9 %all_to_all.10 = bf16[64,24,512]{2,1,0:T(8,128)(2,1)} all-to-all(bf16[64,24,512]{2,1,0:T(8,128)(2,1)S(1)} %bitcast.59), channel_id=1, replica_groups=mesh['dp'=4,'expert'=64] {'expert'}, dimensions={0} | all-to-all | bytes 3145728 | tf_op jit(solution)/shard_map/all_to_all | solution.py:83
  77.5 0.0 all-gather.2.cloned.1.call-update
  77.5 0.2 reduce-scatter.2.cloned.1.call-start
  77.7 0.6 dynamic_slice.11
  78.3 4.7 %fusion.32 = (bf16[1,2048,2,256]{3,2,1,0:T(2,128)(2,1)S(1)}, bf16[1,2048,2,256]{3,2,1,0:T(2,128)(2,1)S(1)}) fusion(bf16[2,2048,2,256]{3,2,1,0:T(2,128)(2,1)} %param.16), kind=kLoop, calls=%fused_computation.77 | loop fusion | bytes 8388608 | tf_op jit(solution)/shard_map/slice | solution.py:86
  83.0 0.5 copy.30
  83.5 1.8 copy.31
  85.4 0.7 fusion.26
  86.0 56.6 %all-gather.2.cloned.1.call-done = bf16[64,24,2048]{2,1,0:T(8,128)(2,1)} async-done(((bf16[64,24,512]{2,1,0:T(8,128)(2,1)}), bf16[64,24,2048]{2,1,0:T(8,128)(2,1)}) %all-gather.2.cloned.1.call-update) | async-done | bytes 6291472 | tf_op jit(solution)/shard_map/all_gather | solution.py:84
  142.6 6.3 %fusion.35 = f32[1536,512]{1,0:T(8,128)S(1)} fusion(bf16[1536,2048]{1,0:T(8,128)(2,1)} %bitcast.71, bf16[2048,512]{1,0:T(8,128)(2,1)} %bitcast.62), kind=kOutput, calls=%fused_computation.80 | convolution fusion | flops 3221225472 | bytes 11534336 | tf_op jit(solution)/shard_map/dot_general | solution.py:24
  148.9 3.5 %fusion.34 = f32[1536,512]{1,0:T(8,128)S(1)} fusion(bf16[1536,2048]{1,0:T(8,128)(2,1)S(1)} %bitcast.72, bf16[2048,512]{1,0:T(8,128)(2,1)S(1)} %bitcast.61), kind=kOutput, calls=%fused_computation.79 | convolution fusion | flops 3221225472 | bytes 11534336 | tf_op jit(solution)/shard_map/dot_general | solution.py:24
  152.4 1.9 convolution_convert_fusion
  154.3 3.9 %broadcast_select_fusion = bf16[1536,2048]{1,0:T(8,128)(2,1)} fusion(bf16[1536,2048]{1,0:T(8,128)(2,1)S(1)} %convolution_convert_fusion, pred[1536]{0:T(1024)(128)(4,1)S(1)} %fusion.26, bf16[2,256,2048]{2,1,0:T(8,128)(2,1)S(1)} %copy-done.8, f32[1536,512]{1,0:T(8,128)S(1)} %fusion.34), kind=kOutput, calls=%fused_computation.6 | convolution fusion | flops 1619263488 | bytes 16779264 | tf_op jit(solution)/shard_map/dot_general | solution.py:32
  158.2 0.0 reduce-scatter.2.cloned.1.call-update
  158.3 67.4 %reduce-scatter.2.cloned.1.call-done = bf16[64,24,512]{2,1,0:T(8,128)(2,1)} async-done(((bf16[64,24,2048]{2,1,0:T(8,128)(2,1)}), bf16[64,24,512]{2,1,0:T(8,128)(2,1)}) %reduce-scatter.2.cloned.1.call-update) | async-done | bytes 1572880 | tf_op jit(solution)/shard_map/reduce_scatter | solution.py:92
  225.7 10.6 %all-to-all-start.1 = ((bf16[64,24,512]{2,1,0:T(8,128)(2,1)}), bf16[64,24,512]{2,1,0:T(8,128)(2,1)S(1)}, u32[]{:S(2)}, u32[]{:S(2)}) async-start(bf16[64,24,512]{2,1,0:T(8,128)(2,1)} %reduce-scatter.2.cloned.1.call-done), calls=%async_computation.2 | async-start | bytes 3145728 | tf_op jit(solution)/shard_map/all_to_all | solution.py:93
  236.3 0.1 copy.25
  236.5 0.1 reshape.274
  236.6 0.3 fusion.33
  236.9 7.0 %gather_fusion.1 = f32[1024]{0:T(1024)S(1)} fusion(f32[128,64]{0,1:T(8,128)S(1)} %fusion.33, s32[1024]{0:T(1024)S(1)} %reshape.274), kind=kCustom, calls=%fused_computation.2 | custom fusion | bytes 16384 | tf_op jit(solution)/shard_map/jit(take_along_axis)/gather | solution.py:62
  243.9 0.1 reshape.277
  244.0 0.1 lt.96
  244.2 0.1 copy.27
  244.3 0.1 copy.28
  244.4 31.7 %all-to-all-done.1 = bf16[64,24,512]{2,1,0:T(8,128)(2,1)S(1)} async-done(((bf16[64,24,512]{2,1,0:T(8,128)(2,1)}), bf16[64,24,512]{2,1,0:T(8,128)(2,1)S(1)}, u32[]{:S(2)}, u32[]{:S(2)}) %all-to-all-start.1) | async-done | bytes 1572896 | tf_op jit(solution)/shard_map/all_to_all | solution.py:93
  276.1 0.1 concatenate.3
  276.2 4.0 %gather_fusion = bf16[1024,512]{1,0:T(8,128)(2,1)S(1)} fusion(bf16[1537,512]{1,0:T(8,128)(2,1)S(1)} %concatenate.3, s32[1024]{0:T(1024)S(1)} %broadcast_clamp_fusion), kind=kCustom, calls=%fused_computation.1 | custom fusion | bytes 2101248 | tf_op jit(solution)/shard_map/gather | solution.py:97
  280.2 0.7 fusion
  280.9 1.6 add_convert_fusion
  (32 shorter events, 0.3 us)
Async XLA Ops:
  6.5 230.0 %copy-start = (bf16[2048,64]{0,1:T(8,128)(2,1)S(1)}, bf16[2048,64]{0,1:T(8,128)(2,1)}, u32[]{:S(2)}) copy-start(bf16[2048,64]{0,1:T(8,128)(2,1)} %param.11) | copy-start | bytes 786436
  6.5 5.9 %copy-start.5 = (s32[128]{0:T(128)S(1)}, s32[128]{0:T(128)}, u32[]{:S(2)}) copy-start(s32[128]{0:T(128)} %param.14) | copy-start | bytes 1540
  6.5 136.1 %all-gather.2.cloned.1.call-start = ((), (), s32[]{:S(2)}) async-start(), calls=%async_computation.3 | async-start | bytes 7864320 | tf_op jit(solution)/shard_map/all_gather | solution.py:84
  11.9 1.5 copy-start.1
  12.7 0.9 copy-start.6
  13.6 0.8 copy-start.2
  77.5 148.1 %reduce-scatter.2.cloned.1.call-start = ((), (), s32[]{:S(2)}) async-start(), calls=%async_computation.4 | async-start | bytes 7864320 | tf_op jit(solution)/shard_map/reduce_scatter | solution.py:92
  142.6 6.3 %copy-start.7 = (bf16[64,24,2048]{2,1,0:T(8,128)(2,1)S(1)}, bf16[64,24,2048]{2,1,0:T(8,128)(2,1)}, u32[]{:S(2)}) copy-start(bf16[64,24,2048]{2,1,0:T(8,128)(2,1)} %all-gather.2.cloned.1.call-done) | copy-start | bytes 18874372
  148.9 3.5 %copy-start.8 = (bf16[2,256,2048]{2,1,0:T(8,128)(2,1)S(1)}, bf16[2,256,2048]{2,1,0:T(8,128)(2,1)}, u32[]{:S(2)}) copy-start(bf16[2,256,2048]{2,1,0:T(8,128)(2,1)} %param.17) | copy-start | bytes 6291460
  158.2 78.1 %copy-start.4 = (s32[128,8]{0,1:T(8,128)S(1)}, s32[128,8]{0,1:T(8,128)}, u32[]{:S(2)}) copy-start(s32[128,8]{0,1:T(8,128)} %param.12) | copy-start | bytes 12292
  158.3 78.3 %copy-start.3 = (bf16[128,2048]{1,0:T(8,128)(2,1)S(1)}, bf16[128,2048]{1,0:T(8,128)(2,1)}, u32[]{:S(2)}) copy-start(bf16[128,2048]{1,0:T(8,128)(2,1)} %copy-done.2) | copy-start | bytes 1572868
  225.7 50.4 %all-to-all-start.1 = ((bf16[64,24,512]{2,1,0:T(8,128)(2,1)}), bf16[64,24,512]{2,1,0:T(8,128)(2,1)S(1)}, u32[]{:S(2)}, u32[]{:S(2)}) async-start(bf16[64,24,512]{2,1,0:T(8,128)(2,1)} %reduce-scatter.2.cloned.1.call-done), calls=%async_computation.2 | async-start | bytes 3145728 | tf_op jit(solution)/shard_map/all_to_all | solution.py:93
Sparse Core Ops, SparseCore 0:
  77.6 64.9 all-gather.1
  158.4 67.2 reduce-scatter.1
where the time goes:
time: 290 us; the launch traced here: 289 us
  waiting for transfers between devices  156 us (54%)
  blocking collectives  52.9 us (18%)
  local copies, waits for them, and re-layouts  32.3 us (11%)
  matrix products  15.8 us (5%)
  between operations  13.8 us (5%)
  starting transfers between devices  10.9 us (4%)
  other arithmetic  7.97 us (3%)
    reduce_scatter x1, waiting for transfers between devices, on_device(): lax.psum_scatter(partial_value, 'dp', scatter_dimension=2, tiled=True)  67.4 us
    all_gather x1, waiting for transfers between devices, on_device(): incoming = lax.all_gather(incoming_part, 'dp', axis=2, tiled=True)  56.6 us
    all_to_all x1, blocking collectives, on_device(): lax.all_to_all(outgoing, 'expert', split_axis=0, concat_axis=0, tiled=True)  52.9 us
    all_to_all x1, waiting for transfers between devices, on_device(): lax.all_to_all(summed, 'expert', split_axis=0, concat_axis=0, tiled=True)  31.7 us
    all_to_all x1, starting transfers between devices, on_device(): lax.all_to_all(summed, 'expert', split_axis=0, concat_axis=0, tiled=True)  10.6 us
    scatter x1, local copies, waits for them, and re-layouts, on_device(): outgoing = jnp.zeros((peer_count * buffer_rows + 1, quarter), jnp.bfloat1...  10.1 us
    dot_general x2, matrix products, slot_partial(): jnp.dot(flat_rows, gate_up_one.reshape(model_width, 2 * unit_count), pref...  9.76 us
    gather x5, local copies, waits for them, and re-layouts, on_device(): jnp.take_along_axis(logits, experts, axis=1)  7.34 us
  transfers between devices with their start and end apart: 3, of which 3 were waited for; matrix products, arithmetic and copies ran while one was open for 6% of the time, Pallas kernels for 0%

commit v1 on v0

--- a/solution.py
+++ b/solution.py
@@ -81,7 +81,14 @@
     )
     outgoing = outgoing[:-1].reshape(peer_count, buffer_rows, quarter)
     incoming_part = lax.all_to_all(outgoing, "expert", split_axis=0, concat_axis=0, tiled=True)
-    incoming = lax.all_gather(incoming_part, "dp", axis=2, tiled=True)
+
+    def do_cubes_all(arr_in):
+        lanes = jax.lax.psum(1, axis_name="dp")
+        seen = [lanes if kk == 2 else 1 for kk in range(arr_in.ndim)]
+        after = jnp.tile(arr_in, seen)
+        return jax.lax.all_to_all(after, axis_name="dp", split_axis=2, concat_axis=2, tiled=True)
+
+    incoming = do_cubes_all(incoming_part)
     flat_in = incoming.reshape(peer_count * buffer_rows, model_width)
     first_out = slot_partial(flat_in, slot_gate_up_weight[0], down_weight[0])
     second_out = slot_partial(flat_in, slot_gate_up_weight[1], down_weight[1])

time: 290 us -> 349 us (1.20)
  local copies, waits for them, and re-layouts: 32.3 us -> 86.2 us
  starting transfers between devices: 10.9 us -> 15.9 us
    all_to_all x0 -> x1, waiting for transfers between devices: none -> 62.9 us  [do_cubes_all(): jax.lax.all_to_all(after, axis_name='dp', split_axis=2, concat_axis=2, ti...]
    all_gather x1 -> x0, waiting for transfers between devices: 56.6 us -> none  [on_device(): incoming = lax.all_gather(incoming_part, 'dp', axis=2, tiled=True)]
    unnamed x22 -> x26, local copies, waits for them, and re-layouts: 4.48 us -> 30.3 us
    all_to_all x0 -> x2, local copies, waits for them, and re-layouts: none -> 22 us  [the longest x1 17.2 us: do_cubes_all(): jax.lax.all_to_all(after, axis_name='dp', split_axis=2, concat_axis=2, ti...]
    another operation x3 -> x4, local copies, waits for them, and re-layouts: 0.28 us -> 6.46 us  [the longest x1 6.19 us: do_cubes_all(): after = jnp.tile(arr_in, seen)]
    reduce_scatter x1, waiting for transfers between devices: 67.4 us -> 61.9 us  [on_device(): lax.psum_scatter(partial_value, 'dp', scatter_dimension=2, tiled=True)]
    all_to_all x0 -> x1, starting transfers between devices: none -> 5.28 us  [do_cubes_all(): jax.lax.all_to_all(after, axis_name='dp', split_axis=2, concat_axis=2, ti...]
  transfers between devices with their start and end apart: 3 -> 3, of which waited for: 3 -> 3; matrix products, arithmetic and copies ran while one was open for 6% -> 5% of each run, Pallas kernels for 0% -> 0%
where the time goes in v1:
time: 349 us; the launch traced here: 348 us
  waiting for transfers between devices  157 us (45%)
  local copies, waits for them, and re-layouts  86.2 us (25%)
  blocking collectives  52.9 us (15%)
  starting transfers between devices  15.9 us (5%)
  matrix products  15.7 us (4%)
  between operations  13.8 us (4%)
  other arithmetic  6.91 us (2%)
    all_to_all x1, waiting for transfers between devices, do_cubes_all(): jax.lax.all_to_all(after, axis_name='dp', split_axis=2, concat_axis=2, ti...  62.9 us
    reduce_scatter x1, waiting for transfers between devices, on_device(): lax.psum_scatter(partial_value, 'dp', scatter_dimension=2, tiled=True)  61.9 us
    all_to_all x1, blocking collectives, on_device(): lax.all_to_all(outgoing, 'expert', split_axis=0, concat_axis=0, tiled=True)  52.9 us
    all_to_all x1, waiting for transfers between devices, on_device(): lax.all_to_all(summed, 'expert', split_axis=0, concat_axis=0, tiled=True)  31.7 us
    unnamed x26, local copies, waits for them, and re-layouts  30.3 us
    all_to_all x1, local copies, waits for them, and re-layouts, do_cubes_all(): jax.lax.all_to_all(after, axis_name='dp', split_axis=2, concat_axis=2, ti...  17.2 us
    all_to_all x1, starting transfers between devices, on_device(): lax.all_to_all(summed, 'expert', split_axis=0, concat_axis=0, tiled=True)  10.6 us
    scatter x1, local copies, waits for them, and re-layouts, on_device(): outgoing = jnp.zeros((peer_count * buffer_rows + 1, quarter), jnp.bfloat1...  10.1 us
  transfers between devices with their start and end apart: 3, of which 3 were waited for; matrix products, arithmetic and copies ran while one was open for 5% of the time, Pallas kernels for 0%

profile of v1, /device:TPU:1, one launch (start us, length us, event | category | flops | bytes accessed | tf_op | source)
XLA Modules:
  0.0 348.0 jit_solution(16013226307849434911)
XLA Ops:
  6.5 0.8 copy.52
  7.4 0.1 eq.65
  7.5 0.8 compare_convert_fusion
  8.2 0.8 convert_reduce_fusion
  9.0 0.8 copy.53
  9.8 0.1 reshape.254
  9.9 0.5 reduce_window_sum.26
  10.4 0.1 add_select_fusion.1
  10.6 0.9 fusion.19
  11.4 0.1 copy.54
  11.5 0.2 fusion.23
  11.8 0.3 copy.55
  12.1 0.2 fusion.3
  12.3 0.2 select_reduce_fusion
  12.5 0.2 fusion.5
  12.8 0.7 copy-done.3
  13.6 10.1 %scatter_custom_fusion = bf16[1537,512]{1,0:T(8,128)(2,1)S(1)} fusion(s32[1024]{0:T(1024)S(1)} %bitcast.75, bf16[128,512]{1,0:T(8,128)(2,1)S(1)} %constant_dynamic-slice_fusion, s32[1024]{0:T(1024)S(1)} %broadcast_clamp_fusion.1, bf16[]{:T(256)} %constant.114.clone.1), kind=kCustom, calls=%fused_computation.20 | custom fusion | bytes 1573890 | tf_op jit(solution)/shard_map/scatter | solution.py:80
  23.7 0.1 slice.52
  23.8 52.9 %all_to_all.15 = bf16[64,24,512]{2,1,0:T(8,128)(2,1)} all-to-all(bf16[64,24,512]{2,1,0:T(8,128)(2,1)S(1)} %bitcast.63), channel_id=1, replica_groups=mesh['dp'=4,'expert'=64] {'expert'}, dimensions={0} | all-to-all | bytes 3145728 | tf_op jit(solution)/shard_map/all_to_all | solution.py:83
  76.7 4.8 %copy.60 = bf16[64,24,512]{0,1,2:T(8,128)(2,1)S(1)} copy(bf16[64,24,512]{2,1,0:T(8,128)(2,1)} %all_to_all.15) | data formatting | bytes 3145728 | tf_op jit(solution)/shard_map/all_to_all | solution.py:83
  81.5 6.2 %tile.4 = bf16[64,24,4,512]{0,1,3,2:T(8,128)(2,1)} broadcast(bf16[64,24,512]{0,1,2:T(8,128)(2,1)S(1)} %copy.60), dimensions={0,1,3} | broadcast | bytes 7864320 | tf_op jit(solution)/shard_map/tile | solution.py:88
  87.7 12.8 %reshape.303 = bf16[4,2,393216]{2,1,0:T(2,128)(2,1)} reshape(bf16[2048,24,64]{2,1,0:T(8,128)(2,1)} %bitcast.59) | data formatting | bytes 12582912
  100.5 5.3 %all-to-all-start.1 = ((bf16[4,2,393216]{2,1,0:T(2,128)(2,1)}), bf16[4,2,393216]{2,1,0:T(2,128)(2,1)}, u32[]{:S(2)}, u32[]{:S(2)}) async-start(bf16[4,2,393216]{2,1,0:T(2,128)(2,1)} %reshape.303), calls=%async_computation.1 | async-start | bytes 12582912 | tf_op jit(solution)/shard_map/all_to_all | solution.py:89
  105.9 4.7 %fusion.32 = (bf16[1,2048,2,256]{3,2,1,0:T(2,128)(2,1)S(1)}, bf16[1,2048,2,256]{3,2,1,0:T(2,128)(2,1)S(1)}) fusion(bf16[2,2048,2,256]{3,2,1,0:T(2,128)(2,1)} %param.16), kind=kLoop, calls=%fused_computation.77 | loop fusion | bytes 8388608 | tf_op jit(solution)/shard_map/slice | solution.py:93
  110.5 0.5 copy.64
  111.1 1.9 copy.63
  113.0 0.6 dynamic_slice.11
  113.6 0.7 fusion.26
  114.2 62.9 %all-to-all-done.1 = bf16[4,2,393216]{2,1,0:T(2,128)(2,1)} async-done(((bf16[4,2,393216]{2,1,0:T(2,128)(2,1)}), bf16[4,2,393216]{2,1,0:T(2,128)(2,1)}, u32[]{:S(2)}, u32[]{:S(2)}) %all-to-all-start.1) | async-done | bytes 6291488 | tf_op jit(solution)/shard_map/all_to_all | solution.py:89
  177.1 12.6 %reshape.304 = bf16[2048,24,64]{2,1,0:T(8,128)(2,1)} reshape(bf16[4,2,393216]{2,1,0:T(2,128)(2,1)} %all-to-all-done.1) | data formatting | bytes 12582912
  189.8 17.2 %copy.61 = bf16[64,24,2048]{2,1,0:T(8,128)(2,1)} copy(bf16[64,24,2048]{0,1,2:T(8,128)(2,1)} %bitcast.58) | data formatting | bytes 12582912 | tf_op jit(solution)/shard_map/all_to_all | solution.py:89
  206.9 6.1 %fusion.35 = f32[1536,512]{1,0:T(8,128)S(1)} fusion(bf16[1536,2048]{1,0:T(8,128)(2,1)} %bitcast.65, bf16[2048,512]{1,0:T(8,128)(2,1)S(1)} %bitcast.67), kind=kOutput, calls=%fused_computation.80 | convolution fusion | flops 3221225472 | bytes 11534336 | tf_op jit(solution)/shard_map/dot_general | solution.py:24
  213.1 3.5 fusion.34
  216.5 1.9 convolution_convert_fusion
  218.4 4.0 %broadcast_select_fusion = bf16[1536,2048]{1,0:T(8,128)(2,1)} fusion(bf16[1536,2048]{1,0:T(8,128)(2,1)S(1)} %convolution_convert_fusion, pred[1536]{0:T(1024)(128)(4,1)S(1)} %fusion.26, bf16[2,256,2048]{2,1,0:T(8,128)(2,1)S(1)} %copy-done.9, f32[1536,512]{1,0:T(8,128)S(1)} %fusion.34), kind=kOutput, calls=%fused_computation.6 | convolution fusion | flops 1619263488 | bytes 16779264 | tf_op jit(solution)/shard_map/dot_general | solution.py:32
  222.5 61.9 %reduce-scatter.2.cloned.1.call-done = bf16[64,24,512]{2,1,0:T(8,128)(2,1)} async-done(((bf16[64,24,2048]{2,1,0:T(8,128)(2,1)}), bf16[64,24,512]{2,1,0:T(8,128)(2,1)}) %reduce-scatter.2.cloned.1.call-update) | async-done | bytes 1572880 | tf_op jit(solution)/shard_map/reduce_scatter | solution.py:99
  284.4 10.6 %all-to-all-start.2 = ((bf16[64,24,512]{2,1,0:T(8,128)(2,1)}), bf16[64,24,512]{2,1,0:T(8,128)(2,1)S(1)}, u32[]{:S(2)}, u32[]{:S(2)}) async-start(bf16[64,24,512]{2,1,0:T(8,128)(2,1)} %reduce-scatter.2.cloned.1.call-done), calls=%async_computation.3 | async-start | bytes 3145728 | tf_op jit(solution)/shard_map/all_to_all | solution.py:100
  295.0 0.1 lt.96
  295.2 0.1 copy.56
  295.3 0.1 reshape.278
  295.4 0.3 fusion.33
  295.7 7.0 %gather_fusion.1 = f32[1024]{0:T(1024)S(1)} fusion(f32[128,64]{0,1:T(8,128)S(1)} %fusion.33, s32[1024]{0:T(1024)S(1)} %reshape.278), kind=kCustom, calls=%fused_computation.2 | custom fusion | bytes 16384 | tf_op jit(solution)/shard_map/jit(take_along_axis)/gather | solution.py:62
  302.9 0.1 copy.59
  303.1 31.7 %all-to-all-done.2 = bf16[64,24,512]{2,1,0:T(8,128)(2,1)S(1)} async-done(((bf16[64,24,512]{2,1,0:T(8,128)(2,1)}), bf16[64,24,512]{2,1,0:T(8,128)(2,1)S(1)}, u32[]{:S(2)}, u32[]{:S(2)}) %all-to-all-start.2) | async-done | bytes 1572896 | tf_op jit(solution)/shard_map/all_to_all | solution.py:100
  334.8 0.1 concatenate.3
  334.9 4.0 %gather_fusion = bf16[1024,512]{1,0:T(8,128)(2,1)S(1)} fusion(bf16[1537,512]{1,0:T(8,128)(2,1)S(1)} %concatenate.3, s32[1024]{0:T(1024)S(1)} %broadcast_clamp_fusion), kind=kCustom, calls=%fused_computation.1 | custom fusion | bytes 2101248 | tf_op jit(solution)/shard_map/gather | solution.py:104
  338.9 0.7 fusion
  339.6 1.6 add_convert_fusion
  (38 shorter events, 0.5 us)
Async XLA Ops:
  6.5 288.9 %copy-start = (bf16[2048,64]{0,1:T(8,128)(2,1)S(1)}, bf16[2048,64]{0,1:T(8,128)(2,1)}, u32[]{:S(2)}) copy-start(bf16[2048,64]{0,1:T(8,128)(2,1)} %param.11) | copy-start | bytes 786436
  9.9 2.2 copy-start.7
  9.9 2.2 copy-start.2
  10.4 1.9 copy-start.8
  12.7 0.8 copy-start.3
  100.5 76.6 %all-to-all-start.1 = ((bf16[4,2,393216]{2,1,0:T(2,128)(2,1)}), bf16[4,2,393216]{2,1,0:T(2,128)(2,1)}, u32[]{:S(2)}, u32[]{:S(2)}) async-start(bf16[4,2,393216]{2,1,0:T(2,128)(2,1)} %reshape.303), calls=%async_computation.1 | async-start | bytes 12582912 | tf_op jit(solution)/shard_map/all_to_all | solution.py:89
  105.8 178.6 %reduce-scatter.2.cloned.1.call-start = ((), (), s32[]{:S(2)}) async-start(), calls=%async_computation.4 | async-start | bytes 7864320 | tf_op jit(solution)/shard_map/reduce_scatter | solution.py:99
  206.9 6.1 %copy-start.1 = (bf16[64,24,2048]{2,1,0:T(8,128)(2,1)S(1)}, bf16[64,24,2048]{2,1,0:T(8,128)(2,1)}, u32[]{:S(2)}) copy-start(bf16[64,24,2048]{2,1,0:T(8,128)(2,1)} %copy.61) | copy-start | bytes 18874372
  206.9 6.1 %copy-start.5 = (bf16[256,8,2,256]{3,1,2,0:T(8,128)(2,1)S(1)}, bf16[256,8,2,256]{3,1,2,0:T(8,128)(2,1)}, u32[]{:S(2)}) copy-start(bf16[256,8,2,256]{3,1,2,0:T(8,128)(2,1)} %copy.63) | copy-start | bytes 6291460
  213.1 3.5 copy-start.9
  222.4 72.7 %copy-start.6 = (s32[128,8]{0,1:T(8,128)S(1)}, s32[128,8]{0,1:T(8,128)}, u32[]{:S(2)}) copy-start(s32[128,8]{0,1:T(8,128)} %param.12) | copy-start | bytes 12292
  222.5 73.0 %copy-start.4 = (bf16[128,2048]{1,0:T(8,128)(2,1)S(1)}, bf16[128,2048]{1,0:T(8,128)(2,1)}, u32[]{:S(2)}) copy-start(bf16[128,2048]{1,0:T(8,128)(2,1)} %copy-done.3) | copy-start | bytes 1572868
  284.4 50.4 %all-to-all-start.2 = ((bf16[64,24,512]{2,1,0:T(8,128)(2,1)}), bf16[64,24,512]{2,1,0:T(8,128)(2,1)S(1)}, u32[]{:S(2)}, u32[]{:S(2)}) async-start(bf16[64,24,512]{2,1,0:T(8,128)(2,1)} %reduce-scatter.2.cloned.1.call-done), calls=%async_computation.3 | async-start | bytes 3145728 | tf_op jit(solution)/shard_map/all_to_all | solution.py:100
Sparse Core Ops, SparseCore 0:
  222.6 61.7 reduce-scatter.1
